TPU v7x, 32 devices: a whole 2x2x4 slice. The times are simulated.
32 devices in a mesh: parts: 2 (over y), slab: 4 (over z), orb: 2 (over x), pen: 2 (over core).
Axes of the slice: x: 2, y: 2, z: 4, core: 2. Of those that a mesh axis runs over, the one named last changes fastest.
Arguments:
- orbitals: float32 [128, 16, 8, 256], P(('parts', 'orb'), 'slab', 'pen'), parts along dimension 0, may hold values from -7.6 to 7.6
- energies: float32 [128], P(('parts', 'orb')), parts along dimension 0, may hold values from -1 to 0.5
- frequency: float32 [2], P('parts'), parts along dimension 0, may hold values from 0.5 to 2
- local_potential: float32 [16, 8, 256], P('slab', 'pen'), may hold values from -1 to 1
- perturbation: float32 [16, 8, 256], P('slab', 'pen'), may hold values from 0.5 to 1.5
- projectors: float32 [128, 8, 256], P(None, 'pen'), may hold values from -0.0625 to 0.0625
- profiles: float32 [128, 5], replicated, may hold values from 0.5 to 2
- couplings: float32 [128], replicated, may hold values from 4 to 12
- atom_planes: int32 [128], replicated, may hold values from 0 to 15
Outputs:
- response_real: float32 [128, 16, 8, 256], P(('parts', 'orb'), 'slab', 'pen'), parts along dimension 0
- density: float32 [32, 8, 256], P(('parts', 'slab'), 'pen'), parts along dimension 0
There are 2 independent parts, one for each index of `parts`. A program takes and returns all parts, laid end to end along the dimension named above; an argument that names none is the same for every part. Nothing has to cross between parts.
Inputs may be any that keep to these rules, and one draw needn't show every extreme that they name: Projector a covers the planes (atom_planes[a] + d) mod 16 of the first dimension for d < 5.
All inputs are finite; a program needn't handle non-finite values.
Results may differ from a plain program's by a relative error of at most 0.0003.
Values sent between devices are 32-bit elements; how exact they have to be, the bound alone decides.
A program may use at most 64 MiB of HBM per device.

v0:
```python
import jax
import jax.numpy as jnp
from jax import lax
from jax.sharding import PartitionSpec as P

NOCC = 64
ITERS = 2
kinetic_scale = 0.125
highest = lax.Precision.HIGHEST


def extended(cells, sides, width):
    for axis, dim in sides:
        count = lax.axis_size(axis)
        head = lax.slice_in_dim(cells, 0, width, axis=dim)
        tail = lax.slice_in_dim(cells, cells.shape[dim] - width, cells.shape[dim], axis=dim)
        cells = jnp.concatenate(
            [
                lax.ppermute(tail, axis, [(i, (i + 1) % count) for i in range(count)]),
                cells,
                lax.ppermute(head, axis, [((i + 1) % count, i) for i in range(count)]),
            ],
            axis=dim,
        )
    return cells


def plane_weights(atom_planes, profiles, planes, depth_total):
    span_size = profiles.shape[1]
    covered = (atom_planes[:, None] + jnp.arange(span_size, dtype=jnp.int32)[None, :]) % depth_total
    matches = (covered[:, :, None] == planes[None, None, :]).astype(jnp.float32)
    return jnp.sum(profiles[:, :, None] * matches, axis=1)


def coefficients(values, projectors, weights, couplings):
    orb_count, plane_count, row_count, col_count = values.shape
    flat_values = values.reshape(orb_count * plane_count, row_count * col_count)
    flat_beta = projectors.reshape(projectors.shape[0], row_count * col_count)
    inner_sums = lax.dot_general(
        flat_beta, flat_values, (((1,), (1,)), ((), ())), precision=highest
    )
    inner_sums = inner_sums.reshape(projectors.shape[0], orb_count, plane_count)
    partial_sum = jnp.einsum("aiz,az->ai", inner_sums, weights, precision=highest)
    summed = lax.psum(partial_sum, ("slab", "pen"))
    return couplings[:, None] * summed


def apply_section(padded, potential, beta_out, weights_out, expansion, energies):
    centre = padded[:, 1:-1, 1:-1]
    beside_all = (
        padded[:, 2:, 1:-1] + padded[:, :-2, 1:-1] + padded[:, 1:-1, 2:] + padded[:, 1:-1, :-2]
    )
    beside_all = beside_all + jnp.roll(centre, 1, 3) + jnp.roll(centre, -1, 3)
    orb_count, plane_count, row_count, col_count = centre.shape
    spread = weights_out[:, None, :] * expansion[:, :, None]
    flat_spread = spread.reshape(spread.shape[0], orb_count * plane_count)
    flat_beta = beta_out.reshape(beta_out.shape[0], row_count * col_count)
    nonlocal_term = lax.dot_general(
        flat_spread, flat_beta, (((0,), (0,)), ((), ())), precision=highest
    )
    nonlocal_term = nonlocal_term.reshape(orb_count, plane_count, row_count, col_count)
    return (
        kinetic_scale * (6.0 * centre - beside_all)
        + potential[None] * centre
        + nonlocal_term
        - energies[:, None, None, None] * centre
    )


def on_device(
    orbitals,
    energies,
    frequency,
    local_potential,
    perturbation,
    projectors,
    profiles,
    couplings,
    atom_planes,
):
    orb_count, plane_count, row_count, col_count = orbitals.shape
    depth_total = plane_count * lax.axis_size("slab")
    cell_total = float(depth_total * row_count * lax.axis_size("pen") * col_count)
    first_plane = lax.axis_index("slab") * plane_count
    planes = (first_plane + jnp.arange(plane_count, dtype=jnp.int32)) % depth_total
    weights = plane_weights(atom_planes, profiles, planes, depth_total)
    freq_square = frequency[0] * frequency[0]
    everyone = lax.all_gather(orbitals, "orb", axis=0, tiled=True)
    every_flat = everyone.reshape(everyone.shape[0], -1)

    def correlation_terms(values):
        return lax.dot_general(
            every_flat, values.reshape(orb_count, -1), (((1,), (1,)), ((), ())), precision=highest
        )

    def removed(values, totals, factor):
        expansion = jax.scipy.linalg.cho_solve((factor, True), totals / cell_total)
        removed_part = lax.dot_general(
            expansion, every_flat, (((0,), (0,)), ((), ())), precision=highest
        )
        return values - removed_part.reshape(values.shape)

    def squares(values):
        return lax.psum(jnp.sum(values * values, axis=(1, 2, 3)), ("slab", "pen"))

    def apply_shallow(values):
        padded = extended(values, (("slab", 1), ("pen", 2)), 1)
        expansion = coefficients(values, projectors, weights, couplings)
        return apply_section(padded, local_potential, projectors, weights, expansion, energies)

    source = perturbation[None] * orbitals
    gram_part = lax.dot_general(every_flat, every_flat, (((1,), (1,)), ((), ())), precision=highest)
    gram_total, source_total = lax.psum((gram_part, correlation_terms(source)), ("slab", "pen"))
    factor = jnp.linalg.cholesky(gram_total / cell_total)
    residual = -removed(source, source_total, factor)
    direction = residual
    solution = jnp.zeros_like(residual)
    norm_now = squares(residual)
    for iteration in range(ITERS):
        direction_total = lax.psum(correlation_terms(direction), ("slab", "pen"))
        inner_field = removed(direction, direction_total, factor)
        first_half = apply_shallow(inner_field)
        second = apply_shallow(first_half)
        first_half, second = (first_half, second)
        target = second + freq_square * inner_field
        curve_part = jnp.sum(first_half * first_half, axis=(1, 2, 3)) + freq_square * jnp.sum(
            inner_field * inner_field, axis=(1, 2, 3)
        )
        image_total, curvature = lax.psum((correlation_terms(target), curve_part), ("slab", "pen"))
        image_field = removed(target, image_total, factor)
        step_size = norm_now / curvature
        solution = solution + step_size[:, None, None, None] * direction
        residual = residual - step_size[:, None, None, None] * image_field
        norm_next = squares(residual)
        direction = residual + (norm_next / norm_now)[:, None, None, None] * direction
        norm_now = norm_next
    padded = extended(solution, (("slab", 1), ("pen", 2)), 1)
    final_expansion = coefficients(solution, projectors, weights, couplings)
    response_real = apply_section(
        padded, local_potential, projectors, weights, final_expansion, energies
    )
    density = lax.psum(jnp.sum(orbitals * response_real, axis=0), "orb") * (4.0 / NOCC)
    return (response_real, density)


def solution(mesh):
    in_specs = (
        P(("parts", "orb"), "slab", "pen", None),
        P(("parts", "orb")),
        P("parts"),
        P("slab", "pen", None),
        P("slab", "pen", None),
        P(None, "pen", None),
        P(),
        P(),
        P(),
    )
    out_specs = (P(("parts", "orb"), "slab", "pen", None), P(("parts", "slab"), "pen", None))
    return jax.shard_map(
        on_device, mesh=mesh, in_specs=in_specs, out_specs=out_specs, check_vma=False
    )
```

profile of v0, /device:TPU:0, one launch (start us, length us, event | category | flops | bytes accessed | tf_op | source)
XLA Modules:
  0.0 372.5 jit_solution(15849839324657514728)
XLA Ops:
  7.2 2.1 copy.40
  12.3 21.8 %all-gather.2.cloned.1.call-done = f32[64,4,4,256]{3,0,2,1:T(8,128)} async-done(((f32[32,4,4,256]{3,0,2,1:T(8,128)}), f32[64,4,4,256]{3,0,2,1:T(8,128)}) %all-gather.2.cloned.1.call-update) | async-done | bytes 1048592 | tf_op jit(solution)/shard_map/all_gather | solution.py:88
  34.1 2.6 convolution_bitcast_fusion
  37.9 28.8 %all-reduce.1 = (f32[64,64]{0,1:T(8,128)S(1)}, f32[64,32]{0,1:T(8,128)S(1)}) all-reduce(f32[64,64]{0,1:T(8,128)S(1)} %convolution_bitcast_fusion, f32[64,32]{0,1:T(8,128)S(1)} %convolution_bitcast_fusion.4), channel_id=1, replica_groups=mesh['parts'=2,'slab'=4,'orb'=2,'pen'=2] {'slab','pen'}, use_global_device_ids=true, to_apply=%region_0.1 | all-reduce | flops 6144 | bytes 49152 | tf_op jit(solution)/shard_map/psum | solution.py:113
  66.8 5.8 %cholesky.18 = f32[64,64]{1,0:T(8,128)S(1)} custom-call(f32[64,64]{1,0:T(8,128)S(1)} %fusion.65), custom_call_target="Cholesky" | custom-call | tf_op jit(solution)/shard_map/jit(cholesky)/cholesky | solution.py:114
  74.0 4.9 %custom-call.11 = f32[1,64,64]{1,2,0:T(8,128)S(1)} custom-call(f32[1,64,64]{2,1,0:T(8,128)S(1)} %fusion.52), custom_call_target="InvertDiagBlocksLowerTriangular" | custom-call | tf_op jit(solution)/shard_map/jit(_cho_solve)/triangular_solve | solution.py:97
  85.9 25.9 %psum.101 = f32[64,32]{0,1:T(8,128)S(1)} all-reduce(f32[64,32]{0,1:T(8,128)S(1)} %convolution_bitcast_fusion.3), channel_id=1, replica_groups=mesh['parts'=2,'slab'=4,'orb'=2,'pen'=2] {'slab','pen'}, use_global_device_ids=true, to_apply=%region_6.8 | all-reduce | flops 2048 | bytes 16384 | tf_op jit(solution)/shard_map/psum | solution.py:120
  116.6 3.8 %collective-permute-start = (f32[32,1,4,256]{3,0,2,1:T(8,128)}, f32[32,1,4,256]{3,0,2,1:T(8,128)}, u32[]{:S(2)}, u32[]{:S(2)}) collective-permute-start(f32[32,1,4,256]{3,0,2,1:T(8,128)} %get-tuple-element.45), channel_id=1, source_target_pairs={{4,0},{8,4},{12,8},{0,12},{5,1},{9,5},{13,9},{1,13},{6,2},{10,6},{... | collective-permute-start | bytes 393224 | tf_op jit(solution)/shard_map/ppermute | solution.py:21
  122.1 25.9 %psum.102 = f32[128,32]{0,1:T(8,128)S(1)} all-reduce(f32[128,32]{0,1:T(8,128)S(1)} %multiply_reduce_fusion.9), channel_id=1, replica_groups=mesh['parts'=2,'slab'=4,'orb'=2,'pen'=2] {'slab','pen'}, use_global_device_ids=true, to_apply=%region_8.10 | all-reduce | flops 4096 | bytes 32768 | tf_op jit(solution)/shard_map/psum | solution.py:44
  151.5 2.2 multiply_reduce_fusion.4
  156.8 3.8 %collective-permute-start.4 = (f32[32,1,4,256]{3,0,2,1:T(8,128)}, f32[32,1,4,256]{3,0,2,1:T(8,128)}, u32[]{:S(2)}, u32[]{:S(2)}) collective-permute-start(f32[32,1,4,256]{3,0,2,1:T(8,128)} %get-tuple-element.39), channel_id=1, source_target_pairs={{4,0},{8,4},{12,8},{0,12},{5,1},{9,5},{13,9},{1,13},{6,2},{10,6},{... | collective-permute-start | bytes 393224 | tf_op jit(solution)/shard_map/ppermute | solution.py:21
  162.3 25.9 %psum.104 = f32[128,32]{0,1:T(8,128)S(1)} all-reduce(f32[128,32]{0,1:T(8,128)S(1)} %multiply_reduce_fusion.8), channel_id=1, replica_groups=mesh['parts'=2,'slab'=4,'orb'=2,'pen'=2] {'slab','pen'}, use_global_device_ids=true, to_apply=%region_12.14 | all-reduce | flops 4096 | bytes 32768 | tf_op jit(solution)/shard_map/psum | solution.py:44
  191.2 2.3 fusion.6
  194.5 26.0 %all-reduce = (f32[64,32]{0,1:T(8,128)S(1)}, f32[32]{0:T(128)S(1)}, f32[32]{0:T(128)S(1)}) all-reduce(f32[64,32]{0,1:T(8,128)S(1)} %convolution_bitcast_fusion.2, f32[32]{0:T(128)S(1)} %get-tuple-element.46, f32[32]{0:T(128)S(1)} %multiply_add_fusion.3), channel_id=1, replica_groups=mesh['parts'=2,'slab'=4,'orb'=2,'pen'=2] {'slab','pen'}, use_global_device_ids=true, to_apply=%region_13.15 | all-reduce | flops 2112 | bytes 16896 | tf_op jit(solution)/shard_map/psum | solution.py:129
  220.9 2.5 multiply_reduce_fusion.2
  223.3 13.6 %psum.106 = f32[32]{0:T(128)S(1)} all-reduce(f32[32]{0:T(128)S(1)} %get-tuple-element.52), channel_id=1, replica_groups=mesh['parts'=2,'slab'=4,'orb'=2,'pen'=2] {'slab','pen'}, use_global_device_ids=true, to_apply=%region_15.17 | all-reduce | flops 32 | bytes 256 | tf_op jit(solution)/shard_map/psum | solution.py:104
  237.9 25.9 %psum.107 = f32[64,32]{0,1:T(8,128)S(1)} all-reduce(f32[64,32]{0,1:T(8,128)S(1)} %convolution_bitcast_fusion.1), channel_id=1, replica_groups=mesh['parts'=2,'slab'=4,'orb'=2,'pen'=2] {'slab','pen'}, use_global_device_ids=true, to_apply=%region_16.18 | all-reduce | flops 2048 | bytes 16384 | tf_op jit(solution)/shard_map/psum | solution.py:120
  268.6 3.8 %collective-permute-start.8 = (f32[32,1,4,256]{3,0,2,1:T(8,128)}, f32[32,1,4,256]{3,0,2,1:T(8,128)}, u32[]{:S(2)}, u32[]{:S(2)}) collective-permute-start(f32[32,1,4,256]{3,0,2,1:T(8,128)} %get-tuple-element.33), channel_id=1, source_target_pairs={{4,0},{8,4},{12,8},{0,12},{5,1},{9,5},{13,9},{1,13},{6,2},{10,6},{... | collective-permute-start | bytes 393224 | tf_op jit(solution)/shard_map/ppermute | solution.py:21
  274.1 26.1 %psum.108 = f32[128,32]{0,1:T(8,128)S(1)} all-reduce(f32[128,32]{0,1:T(8,128)S(1)} %multiply_reduce_fusion.7), channel_id=1, replica_groups=mesh['parts'=2,'slab'=4,'orb'=2,'pen'=2] {'slab','pen'}, use_global_device_ids=true, to_apply=%region_17.19 | all-reduce | flops 4096 | bytes 32768 | tf_op jit(solution)/shard_map/psum | solution.py:44
  303.0 2.2 fusion.8
  305.2 13.8 %psum.109 = f32[32]{0:T(128)S(1)} all-reduce(f32[32]{0:T(128)S(1)} %multiply_add_fusion.2), channel_id=1, replica_groups=mesh['parts'=2,'slab'=4,'orb'=2,'pen'=2] {'slab','pen'}, use_global_device_ids=true, to_apply=%region_20.22 | all-reduce | flops 32 | bytes 256 | tf_op jit(solution)/shard_map/psum | solution.py:129
  321.4 3.8 %collective-permute-start.12 = (f32[32,1,4,256]{3,0,2,1:T(8,128)}, f32[32,1,4,256]{3,0,2,1:T(8,128)}, u32[]{:S(2)}, u32[]{:S(2)}) collective-permute-start(f32[32,1,4,256]{3,0,2,1:T(8,128)} %get-tuple-element.27), channel_id=1, source_target_pairs={{4,0},{8,4},{12,8},{0,12},{5,1},{9,5},{13,9},{1,13},{6,2},{10,6},{... | collective-permute-start | bytes 393224 | tf_op jit(solution)/shard_map/ppermute | solution.py:21
  326.0 25.9 %psum.110 = f32[128,32]{0,1:T(8,128)S(1)} all-reduce(f32[128,32]{0,1:T(8,128)S(1)} %multiply_reduce_fusion.6), channel_id=1, replica_groups=mesh['parts'=2,'slab'=4,'orb'=2,'pen'=2] {'slab','pen'}, use_global_device_ids=true, to_apply=%region_21.23 | all-reduce | flops 4096 | bytes 32768 | tf_op jit(solution)/shard_map/psum | solution.py:44
  356.7 7.2 %psum.111 = f32[4,4,256]{2,1,0:T(4,128)S(1)} all-reduce(f32[4,4,256]{2,1,0:T(4,128)S(1)} %get-tuple-element.56), channel_id=1, replica_groups=mesh['parts'=2,'slab'=4,'orb'=2,'pen'=2] {'orb'}, use_global_device_ids=true, to_apply=%region_23.25 | all-reduce | flops 4096 | bytes 32768 | tf_op jit(solution)/shard_map/psum | solution.py:142
  (156 shorter events, 50.4 us)
Async XLA Ops:
  7.2 27.0 %all-gather.2.cloned.1.call-start = ((), (), s32[]{:S(2)}) async-start(), calls=%async_computation | async-start | bytes 1572864 | tf_op jit(solution)/shard_map/all_gather | solution.py:88
  12.3 24.4 %copy-start.7 = (f32[32,4,4,256]{3,2,1,0:T(4,128)S(1)}, f32[32,4,4,256]{3,2,1,0:T(4,128)}, u32[]{:S(2)}) copy-start(f32[32,4,4,256]{3,2,1,0:T(4,128)} %param.11) | copy-start | bytes 1572868
  12.3 24.4 %copy-start.18 = (f32[4,4,256]{2,1,0:T(4,128)S(1)}, f32[4,4,256]{2,1,0:T(4,128)}, u32[]{:S(2)}) copy-start(f32[4,4,256]{2,1,0:T(4,128)} %param.15) | copy-start | bytes 49156
  116.6 31.5 %collective-permute-start.1 = (f32[32,1,4,256]{3,0,2,1:T(8,128)}, f32[32,1,4,256]{3,0,2,1:T(8,128)}, u32[]{:S(2)}, u32[]{:S(2)}) collective-permute-start(f32[32,1,4,256]{3,0,2,1:T(8,128)} %get-tuple-element.44), channel_id=1, source_target_pairs={{0,4},{4,8},{8,12},{12,0},{1,5},{5,9},{9,13},{13,1},{2,6},{6,10},{... | collective-permute-start | bytes 393224 | tf_op jit(solution)/shard_map/ppermute | solution.py:19
  116.6 31.5 %collective-permute-start = (f32[32,1,4,256]{3,0,2,1:T(8,128)}, f32[32,1,4,256]{3,0,2,1:T(8,128)}, u32[]{:S(2)}, u32[]{:S(2)}) collective-permute-start(f32[32,1,4,256]{3,0,2,1:T(8,128)} %get-tuple-element.45), channel_id=1, source_target_pairs={{4,0},{8,4},{12,8},{0,12},{5,1},{9,5},{13,9},{1,13},{6,2},{10,6},{... | collective-permute-start | bytes 393224 | tf_op jit(solution)/shard_map/ppermute | solution.py:21
  122.1 25.9 %copy-start.19 = (f32[128]{0:T(128)S(1)}, f32[128]{0:T(128)}, u32[]{:S(2)}) copy-start(f32[128]{0:T(128)} %param.18) | copy-start | bytes 1540
  148.1 2.8 copy-start.11
  149.0 1.5 collective-permute-start.2
  149.1 1.7 collective-permute-start.3
  156.8 31.5 %collective-permute-start.5 = (f32[32,1,4,256]{3,0,2,1:T(8,128)}, f32[32,1,4,256]{3,0,2,1:T(8,128)}, u32[]{:S(2)}, u32[]{:S(2)}) collective-permute-start(f32[32,1,4,256]{3,0,2,1:T(8,128)} %get-tuple-element.38), channel_id=1, source_target_pairs={{0,4},{4,8},{8,12},{12,0},{1,5},{5,9},{9,13},{13,1},{2,6},{6,10},{... | collective-permute-start | bytes 393224 | tf_op jit(solution)/shard_map/ppermute | solution.py:19
  156.8 31.5 %collective-permute-start.4 = (f32[32,1,4,256]{3,0,2,1:T(8,128)}, f32[32,1,4,256]{3,0,2,1:T(8,128)}, u32[]{:S(2)}, u32[]{:S(2)}) collective-permute-start(f32[32,1,4,256]{3,0,2,1:T(8,128)} %get-tuple-element.39), channel_id=1, source_target_pairs={{4,0},{8,4},{12,8},{0,12},{5,1},{9,5},{13,9},{1,13},{6,2},{10,6},{... | collective-permute-start | bytes 393224 | tf_op jit(solution)/shard_map/ppermute | solution.py:21
  188.2 3.0 copy-start.16
  188.2 3.0 copy-start.6
  188.2 3.0 copy-start.12
  189.4 1.5 collective-permute-start.6
  189.5 1.7 collective-permute-start.7
  268.6 31.6 %collective-permute-start.9 = (f32[32,1,4,256]{3,0,2,1:T(8,128)}, f32[32,1,4,256]{3,0,2,1:T(8,128)}, u32[]{:S(2)}, u32[]{:S(2)}) collective-permute-start(f32[32,1,4,256]{3,0,2,1:T(8,128)} %get-tuple-element.32), channel_id=1, source_target_pairs={{0,4},{4,8},{8,12},{12,0},{1,5},{5,9},{9,13},{13,1},{2,6},{6,10},{... | collective-permute-start | bytes 393224 | tf_op jit(solution)/shard_map/ppermute | solution.py:19
  268.6 31.7 %collective-permute-start.8 = (f32[32,1,4,256]{3,0,2,1:T(8,128)}, f32[32,1,4,256]{3,0,2,1:T(8,128)}, u32[]{:S(2)}, u32[]{:S(2)}) collective-permute-start(f32[32,1,4,256]{3,0,2,1:T(8,128)} %get-tuple-element.33), channel_id=1, source_target_pairs={{4,0},{8,4},{12,8},{0,12},{5,1},{9,5},{13,9},{1,13},{6,2},{10,6},{... | collective-permute-start | bytes 393224 | tf_op jit(solution)/shard_map/ppermute | solution.py:21
  301.2 1.5 collective-permute-start.10
  301.3 1.7 collective-permute-start.11
  321.4 30.5 %collective-permute-start.13 = (f32[32,1,4,256]{3,0,2,1:T(8,128)}, f32[32,1,4,256]{3,0,2,1:T(8,128)}, u32[]{:S(2)}, u32[]{:S(2)}) collective-permute-start(f32[32,1,4,256]{3,0,2,1:T(8,128)} %get-tuple-element.26), channel_id=1, source_target_pairs={{0,4},{4,8},{8,12},{12,0},{1,5},{5,9},{9,13},{13,1},{2,6},{6,10},{... | collective-permute-start | bytes 393224 | tf_op jit(solution)/shard_map/ppermute | solution.py:19
  321.4 30.5 %collective-permute-start.12 = (f32[32,1,4,256]{3,0,2,1:T(8,128)}, f32[32,1,4,256]{3,0,2,1:T(8,128)}, u32[]{:S(2)}, u32[]{:S(2)}) collective-permute-start(f32[32,1,4,256]{3,0,2,1:T(8,128)} %get-tuple-element.27), channel_id=1, source_target_pairs={{4,0},{8,4},{12,8},{0,12},{5,1},{9,5},{13,9},{1,13},{6,2},{10,6},{... | collective-permute-start | bytes 393224 | tf_op jit(solution)/shard_map/ppermute | solution.py:21
  352.8 1.5 collective-permute-start.14
  352.9 1.7 collective-permute-start.15
  (17 other events, 28.6 us)
Sparse Core Ops, SparseCore 0:
  10.1 23.9 all-gather.1
where the time goes:
time: 373 us; the launch traced here: 372 us
  blocking collectives  245 us (66%)
  waiting for transfers between devices  26.6 us (7%)
  matrix products  25.8 us (7%)
  local copies, waits for them, and re-layouts  24.9 us (7%)
  starting transfers between devices  17.6 us (5%)
  other arithmetic  17.1 us (5%)
  between operations  15.3 us (4%)
    psum x4, blocking collectives, coefficients(): summed = lax.psum(partial_sum, ('slab', 'pen'))  104 us
    psum x2, blocking collectives, on_device(): direction_total = lax.psum(correlation_terms(direction), ('slab', 'pen'))  51.8 us
    psum x2, blocking collectives, on_device(): lax.psum((correlation_terms(target), curve_part), ('slab', 'pen'))  39.8 us
    psum x1, blocking collectives, on_device(): lax.psum((gram_part, correlation_terms(source)), ('slab', 'pen'))  28.8 us
    all_gather x1, waiting for transfers between devices, on_device(): everyone = lax.all_gather(orbitals, 'orb', axis=0, tiled=True)  21.8 us
    ppermute x8, starting transfers between devices, extended(): lax.ppermute(head, axis, [((i + 1) % count, i) for i in range(count)])  15.6 us
    psum x1, blocking collectives, squares(): return lax.psum(jnp.sum(values * values, axis=(1, 2, 3)), ('slab', 'pen'))  13.6 us
    dot_general x4, matrix products, apply_section(): lax.dot_general(flat_spread, flat_beta, (((0,), (0,)), ((), ())), precisi...  8.76 us
  transfers between devices with their start and end apart: 17, of which 9 were waited for; matrix products, arithmetic and copies ran while one was open for 1% of the time, Pallas kernels for 0%

commit v1 on v0

--- a/solution.py
+++ b/solution.py
@@ -2,6 +2,7 @@
 import jax.numpy as jnp
 from jax import lax
 from jax.sharding import PartitionSpec as P
+from jax.lax import all_gather
 
 NOCC = 64
 ITERS = 2
@@ -41,7 +42,7 @@
     )
     inner_sums = inner_sums.reshape(projectors.shape[0], orb_count, plane_count)
     partial_sum = jnp.einsum("aiz,az->ai", inner_sums, weights, precision=highest)
-    summed = lax.psum(partial_sum, ("slab", "pen"))
+    summed = jnp.sum(all_gather(partial_sum, axis_name=("slab", "pen")), axis=0)
     return couplings[:, None] * summed
 
 

time: 373 us -> 312 us (0.84)
  blocking collectives: 245 us -> 198 us
  local copies, waits for them, and re-layouts: 24.9 us -> 14.2 us
    psum x4 -> x0, blocking collectives: 104 us -> none  [coefficients(): summed = lax.psum(partial_sum, ('slab', 'pen'))]
    all_gather x0 -> x4, blocking collectives: none -> 56.1 us  [coefficients(): summed = jnp.sum(all_gather(partial_sum, axis_name=('slab', 'pen')), axis=0)]
    slice x8, local copies, waits for them, and re-layouts: 7.01 us -> 1.38 us  [apply_section(): beside_all = beside_all + jnp.roll(centre, 1, 3) + jnp.roll(centre, -1, 3)]
    dot_general x4, matrix products: 8.76 us -> 4.56 us  [apply_section(): lax.dot_general(flat_spread, flat_beta, (((0,), (0,)), ((), ())), precisi...]
    slice x4, other arithmetic: 3.87 us -> 0.11 us  [extended(): head = lax.slice_in_dim(cells, 0, width, axis=dim)]
    unnamed x55 -> x39, local copies, waits for them, and re-layouts: 8.29 us -> 6.13 us
where the time goes in v1:
time: 312 us; the launch traced here: 311 us
  blocking collectives  198 us (63%)
  waiting for transfers between devices  26.9 us (9%)
  matrix products  25.6 us (8%)
  starting transfers between devices  18 us (6%)
  between operations  15.4 us (5%)
  local copies, waits for them, and re-layouts  14.2 us (5%)
  other arithmetic  13.5 us (4%)
    all_gather x4, blocking collectives, coefficients(): summed = jnp.sum(all_gather(partial_sum, axis_name=('slab', 'pen')), axis=0)  56.1 us
    psum x2, blocking collectives, on_device(): direction_total = lax.psum(correlation_terms(direction), ('slab', 'pen'))  51.8 us
    psum x2, blocking collectives, on_device(): lax.psum((correlation_terms(target), curve_part), ('slab', 'pen'))  40.2 us
    psum x1, blocking collectives, on_device(): lax.psum((gram_part, correlation_terms(source)), ('slab', 'pen'))  28.8 us
    all_gather x1, waiting for transfers between devices, on_device(): everyone = lax.all_gather(orbitals, 'orb', axis=0, tiled=True)  21.8 us
    ppermute x8, starting transfers between devices, extended(): lax.ppermute(head, axis, [((i + 1) % count, i) for i in range(count)])  16.9 us
    psum x1, blocking collectives, squares(): return lax.psum(jnp.sum(values * values, axis=(1, 2, 3)), ('slab', 'pen'))  13.6 us
    dot_general x4, matrix products, removed(): lax.dot_general(expansion, every_flat, (((0,), (0,)), ((), ())), precisio...  9.74 us
  transfers between devices with their start and end apart: 17, of which 9 were waited for; matrix products, arithmetic and copies ran while one was open for 1% of the time, Pallas kernels for 0%

profile of v1, /device:TPU:0, one launch (start us, length us, event | category | flops | bytes accessed | tf_op | source)
XLA Modules:
  0.0 311.3 jit_solution(11323838430378516785)
XLA Ops:
  7.2 2.1 copy.60
  12.3 21.8 %all-gather.6.cloned.1.call-done = f32[64,4,4,256]{3,0,2,1:T(8,128)} async-done(((f32[32,4,4,256]{3,0,2,1:T(8,128)}), f32[64,4,4,256]{3,0,2,1:T(8,128)}) %all-gather.6.cloned.1.call-update) | async-done | bytes 1048592 | tf_op jit(solution)/shard_map/all_gather | solution.py:89
  34.1 2.6 convolution_bitcast_fusion
  37.9 28.8 %all-reduce.1 = (f32[64,64]{0,1:T(8,128)S(1)}, f32[64,32]{0,1:T(8,128)S(1)}) all-reduce(f32[64,64]{0,1:T(8,128)S(1)} %convolution_bitcast_fusion, f32[64,32]{0,1:T(8,128)S(1)} %convolution_bitcast_fusion.4), channel_id=1, replica_groups=mesh['parts'=2,'slab'=4,'orb'=2,'pen'=2] {'slab','pen'}, use_global_device_ids=true, to_apply=%region_0.1 | all-reduce | flops 6144 | bytes 49152 | tf_op jit(solution)/shard_map/psum | solution.py:114
  66.8 5.8 %cholesky.18 = f32[64,64]{1,0:T(8,128)S(1)} custom-call(f32[64,64]{1,0:T(8,128)S(1)} %fusion.65), custom_call_target="Cholesky" | custom-call | tf_op jit(solution)/shard_map/jit(cholesky)/cholesky | solution.py:115
  74.0 4.9 %custom-call.11 = f32[1,64,64]{1,2,0:T(8,128)S(1)} custom-call(f32[1,64,64]{2,1,0:T(8,128)S(1)} %fusion.52), custom_call_target="InvertDiagBlocksLowerTriangular" | custom-call | tf_op jit(solution)/shard_map/jit(_cho_solve)/triangular_solve | solution.py:98
  83.4 2.6 multiply_reduce_fusion.5
  87.0 25.9 %psum.73 = f32[64,32]{0,1:T(8,128)S(1)} all-reduce(f32[64,32]{0,1:T(8,128)S(1)} %convolution_bitcast_fusion.3), channel_id=1, replica_groups=mesh['parts'=2,'slab'=4,'orb'=2,'pen'=2] {'slab','pen'}, use_global_device_ids=true, to_apply=%region_6.8 | all-reduce | flops 2048 | bytes 16384 | tf_op jit(solution)/shard_map/psum | solution.py:121
  115.6 3.8 %collective-permute-start = (f32[32,1,4,256]{3,0,2,1:T(8,128)S(1)}, f32[32,1,4,256]{3,0,2,1:T(8,128)S(1)}, u32[]{:S(2)}, u32[]{:S(2)}) collective-permute-start(f32[32,1,4,256]{3,0,2,1:T(8,128)S(1)} %get-tuple-element.47), channel_id=1, source_target_pairs={{4,0},{8,4},{12,8},{0,12},{5,1},{9,5},{13,9},{1,13},{6,2},{10,6},{... | collective-permute-start | bytes 393224 | tf_op jit(solution)/shard_map/ppermute | solution.py:22
  120.2 14.0 %all-gather = f32[1024,32]{0,1:T(8,128)S(1)} all-gather(f32[128,32]{0,1:T(8,128)S(1)} %multiply_reduce_fusion.9), channel_id=2, replica_groups=mesh['parts'=2,'slab'=4,'orb'=2,'pen'=2] {'slab','pen'}, dimensions={0}, use_global_device_ids=true | all-gather | bytes 147456 | tf_op jit(solution)/shard_map/all_gather | solution.py:45
  139.4 3.8 %collective-permute-start.4 = (f32[32,1,4,256]{3,0,2,1:T(8,128)S(1)}, f32[32,1,4,256]{3,0,2,1:T(8,128)S(1)}, u32[]{:S(2)}, u32[]{:S(2)}) collective-permute-start(f32[32,1,4,256]{3,0,2,1:T(8,128)S(1)} %get-tuple-element.41), channel_id=1, source_target_pairs={{4,0},{8,4},{12,8},{0,12},{5,1},{9,5},{13,9},{1,13},{6,2},{10,6},{... | collective-permute-start | bytes 393224 | tf_op jit(solution)/shard_map/ppermute | solution.py:22
  143.9 14.0 %all-gather.1 = f32[1024,32]{0,1:T(8,128)S(1)} all-gather(f32[128,32]{0,1:T(8,128)S(1)} %multiply_reduce_fusion.8), channel_id=3, replica_groups=mesh['parts'=2,'slab'=4,'orb'=2,'pen'=2] {'slab','pen'}, dimensions={0}, use_global_device_ids=true | all-gather | bytes 147456 | tf_op jit(solution)/shard_map/all_gather | solution.py:45
  162.0 26.3 %all-reduce = (f32[64,32]{0,1:T(8,128)S(1)}, f32[32]{0:T(128)S(1)}, f32[32]{0:T(128)S(1)}) all-reduce(f32[64,32]{0,1:T(8,128)S(1)} %convolution_bitcast_fusion.2, f32[32]{0:T(128)S(1)} %get-tuple-element.48, f32[32]{0:T(128)S(1)} %multiply_add_fusion.3), channel_id=1, replica_groups=mesh['parts'=2,'slab'=4,'orb'=2,'pen'=2] {'slab','pen'}, use_global_device_ids=true, to_apply=%region_13.15 | all-reduce | flops 2112 | bytes 16896 | tf_op jit(solution)/shard_map/psum | solution.py:130
  188.6 3.3 %multiply_reduce_fusion.2 = (f32[32]{0:T(128)S(1)}, f32[32,4,4,256]{3,0,2,1:T(8,128)}) fusion(f32[32,4,4,256]{3,0,2,1:T(8,128)} %copy-done.4, f32[64,32,1,1]{0,1,3,2:T(8,128)S(1)} %convolution_bitcast_fusion.6, f32[4,4,256,64]{2,1,0,3:T(4,128)S(1)} %dot_general.107, f32[32]{0:T(128)S(1)} %div.41, f32[32,4,4,256]{3,0,2,1:T(8,128)S(1)} %get-tuple-element.49), kind=kOutput, calls=%fused_computation.98 | convolution fusion | flops 101449696 | bytes 2629888 | tf_op jit(solution)/shard_map/dot_general | solution.py:99
  191.9 13.6 %psum.76 = f32[32]{0:T(128)S(1)} all-reduce(f32[32]{0:T(128)S(1)} %get-tuple-element.54), channel_id=1, replica_groups=mesh['parts'=2,'slab'=4,'orb'=2,'pen'=2] {'slab','pen'}, use_global_device_ids=true, to_apply=%region_15.17 | all-reduce | flops 32 | bytes 256 | tf_op jit(solution)/shard_map/psum | solution.py:105
  205.5 2.0 convolution_bitcast_fusion.1
  207.5 25.9 %psum.77 = f32[64,32]{0,1:T(8,128)S(1)} all-reduce(f32[64,32]{0,1:T(8,128)S(1)} %convolution_bitcast_fusion.1), channel_id=1, replica_groups=mesh['parts'=2,'slab'=4,'orb'=2,'pen'=2] {'slab','pen'}, use_global_device_ids=true, to_apply=%region_16.18 | all-reduce | flops 2048 | bytes 16384 | tf_op jit(solution)/shard_map/psum | solution.py:121
  233.7 2.5 multiply_reduce_fusion.1
  237.0 3.8 %collective-permute-start.8 = (f32[32,1,4,256]{3,0,2,1:T(8,128)S(1)}, f32[32,1,4,256]{3,0,2,1:T(8,128)S(1)}, u32[]{:S(2)}, u32[]{:S(2)}) collective-permute-start(f32[32,1,4,256]{3,0,2,1:T(8,128)S(1)} %get-tuple-element.35), channel_id=1, source_target_pairs={{4,0},{8,4},{12,8},{0,12},{5,1},{9,5},{13,9},{1,13},{6,2},{10,6},{... | collective-permute-start | bytes 393224 | tf_op jit(solution)/shard_map/ppermute | solution.py:22
  241.6 14.2 %all-gather.2 = f32[1024,32]{0,1:T(8,128)S(1)} all-gather(f32[128,32]{0,1:T(8,128)S(1)} %multiply_reduce_fusion.7), channel_id=4, replica_groups=mesh['parts'=2,'slab'=4,'orb'=2,'pen'=2] {'slab','pen'}, dimensions={0}, use_global_device_ids=true | all-gather | bytes 147456 | tf_op jit(solution)/shard_map/all_gather | solution.py:45
  258.8 13.9 %psum.78 = f32[32]{0:T(128)S(1)} all-reduce(f32[32]{0:T(128)S(1)} %multiply_add_fusion.2), channel_id=1, replica_groups=mesh['parts'=2,'slab'=4,'orb'=2,'pen'=2] {'slab','pen'}, use_global_device_ids=true, to_apply=%region_20.22 | all-reduce | flops 32 | bytes 256 | tf_op jit(solution)/shard_map/psum | solution.py:130
  273.7 3.8 %collective-permute-start.12 = (f32[32,1,4,256]{3,0,2,1:T(8,128)S(1)}, f32[32,1,4,256]{3,0,2,1:T(8,128)S(1)}, u32[]{:S(2)}, u32[]{:S(2)}) collective-permute-start(f32[32,1,4,256]{3,0,2,1:T(8,128)S(1)} %get-tuple-element.29), channel_id=1, source_target_pairs={{4,0},{8,4},{12,8},{0,12},{5,1},{9,5},{13,9},{1,13},{6,2},{10,6},{... | collective-permute-start | bytes 393224 | tf_op jit(solution)/shard_map/ppermute | solution.py:22
  278.2 14.0 %all-gather.3 = f32[1024,32]{0,1:T(8,128)S(1)} all-gather(f32[128,32]{0,1:T(8,128)S(1)} %multiply_reduce_fusion.6), channel_id=5, replica_groups=mesh['parts'=2,'slab'=4,'orb'=2,'pen'=2] {'slab','pen'}, dimensions={0}, use_global_device_ids=true | all-gather | bytes 147456 | tf_op jit(solution)/shard_map/all_gather | solution.py:45
  295.5 7.2 %psum.79 = f32[4,4,256]{2,1,0:T(4,128)S(1)} all-reduce(f32[4,4,256]{2,1,0:T(4,128)S(1)} %get-tuple-element.58), channel_id=1, replica_groups=mesh['parts'=2,'slab'=4,'orb'=2,'pen'=2] {'orb'}, use_global_device_ids=true, to_apply=%region_23.25 | all-reduce | flops 4096 | bytes 32768 | tf_op jit(solution)/shard_map/psum | solution.py:143
  (144 shorter events, 35.3 us)
Async XLA Ops:
  7.2 27.0 %all-gather.6.cloned.1.call-start = ((), (), s32[]{:S(2)}) async-start(), calls=%async_computation | async-start | bytes 1572864 | tf_op jit(solution)/shard_map/all_gather | solution.py:89
  12.3 24.4 %copy-start.2 = (f32[32,4,4,256]{3,2,1,0:T(4,128)S(1)}, f32[32,4,4,256]{3,2,1,0:T(4,128)}, u32[]{:S(2)}) copy-start(f32[32,4,4,256]{3,2,1,0:T(4,128)} %param.11) | copy-start | bytes 1572868
  12.3 24.5 %copy-start.8 = (f32[4,4,256]{2,1,0:T(4,128)S(1)}, f32[4,4,256]{2,1,0:T(4,128)}, u32[]{:S(2)}) copy-start(f32[4,4,256]{2,1,0:T(4,128)} %param.15) | copy-start | bytes 49156
  34.1 2.6 copy-start
  115.4 19.5 %collective-permute-start.1 = (f32[32,1,4,256]{3,0,2,1:T(8,128)S(1)}, f32[32,1,4,256]{3,0,2,1:T(8,128)S(1)}, u32[]{:S(2)}, u32[]{:S(2)}) collective-permute-start(f32[32,1,4,256]{3,0,2,1:T(8,128)S(1)} %get-tuple-element.46), channel_id=1, source_target_pairs={{0,4},{4,8},{8,12},{12,0},{1,5},{5,9},{9,13},{13,1},{2,6},{6,10},{... | collective-permute-start | bytes 393224 | tf_op jit(solution)/shard_map/ppermute | solution.py:20
  115.6 19.3 %collective-permute-start = (f32[32,1,4,256]{3,0,2,1:T(8,128)S(1)}, f32[32,1,4,256]{3,0,2,1:T(8,128)S(1)}, u32[]{:S(2)}, u32[]{:S(2)}) collective-permute-start(f32[32,1,4,256]{3,0,2,1:T(8,128)S(1)} %get-tuple-element.47), channel_id=1, source_target_pairs={{4,0},{8,4},{12,8},{0,12},{5,1},{9,5},{13,9},{1,13},{6,2},{10,6},{... | collective-permute-start | bytes 393224 | tf_op jit(solution)/shard_map/ppermute | solution.py:22
  134.8 1.9 copy-start.6
  134.9 1.5 collective-permute-start.2
  135.3 1.4 collective-permute-start.3
  139.3 18.7 %collective-permute-start.5 = (f32[32,1,4,256]{3,0,2,1:T(8,128)S(1)}, f32[32,1,4,256]{3,0,2,1:T(8,128)S(1)}, u32[]{:S(2)}, u32[]{:S(2)}) collective-permute-start(f32[32,1,4,256]{3,0,2,1:T(8,128)S(1)} %get-tuple-element.40), channel_id=1, source_target_pairs={{0,4},{4,8},{8,12},{12,0},{1,5},{5,9},{9,13},{13,1},{2,6},{6,10},{... | collective-permute-start | bytes 393224 | tf_op jit(solution)/shard_map/ppermute | solution.py:20
  139.4 18.6 %collective-permute-start.4 = (f32[32,1,4,256]{3,0,2,1:T(8,128)S(1)}, f32[32,1,4,256]{3,0,2,1:T(8,128)S(1)}, u32[]{:S(2)}, u32[]{:S(2)}) collective-permute-start(f32[32,1,4,256]{3,0,2,1:T(8,128)S(1)} %get-tuple-element.41), channel_id=1, source_target_pairs={{4,0},{8,4},{12,8},{0,12},{5,1},{9,5},{13,9},{1,13},{6,2},{10,6},{... | collective-permute-start | bytes 393224 | tf_op jit(solution)/shard_map/ppermute | solution.py:22
  158.0 1.5 collective-permute-start.6
  158.4 1.4 collective-permute-start.7
  236.9 18.9 %collective-permute-start.9 = (f32[32,1,4,256]{3,0,2,1:T(8,128)S(1)}, f32[32,1,4,256]{3,0,2,1:T(8,128)S(1)}, u32[]{:S(2)}, u32[]{:S(2)}) collective-permute-start(f32[32,1,4,256]{3,0,2,1:T(8,128)S(1)} %get-tuple-element.34), channel_id=1, source_target_pairs={{0,4},{4,8},{8,12},{12,0},{1,5},{5,9},{9,13},{13,1},{2,6},{6,10},{... | collective-permute-start | bytes 393224 | tf_op jit(solution)/shard_map/ppermute | solution.py:20
  237.0 18.8 %collective-permute-start.8 = (f32[32,1,4,256]{3,0,2,1:T(8,128)S(1)}, f32[32,1,4,256]{3,0,2,1:T(8,128)S(1)}, u32[]{:S(2)}, u32[]{:S(2)}) collective-permute-start(f32[32,1,4,256]{3,0,2,1:T(8,128)S(1)} %get-tuple-element.35), channel_id=1, source_target_pairs={{4,0},{8,4},{12,8},{0,12},{5,1},{9,5},{13,9},{1,13},{6,2},{10,6},{... | collective-permute-start | bytes 393224 | tf_op jit(solution)/shard_map/ppermute | solution.py:22
  255.8 1.9 copy-start.7
  255.9 1.5 collective-permute-start.10
  256.3 1.4 collective-permute-start.11
  257.8 14.9 %copy-start.1 = (f32[32,4,4,256]{3,0,2,1:T(8,128)S(1)}, f32[32,4,4,256]{3,0,2,1:T(8,128)}, u32[]{:S(2)}) copy-start(f32[32,4,4,256]{3,0,2,1:T(8,128)} %get-tuple-element.55) | copy-start | bytes 1572868
  273.6 18.7 %collective-permute-start.13 = (f32[32,1,4,256]{3,0,2,1:T(8,128)S(1)}, f32[32,1,4,256]{3,0,2,1:T(8,128)S(1)}, u32[]{:S(2)}, u32[]{:S(2)}) collective-permute-start(f32[32,1,4,256]{3,0,2,1:T(8,128)S(1)} %get-tuple-element.28), channel_id=1, source_target_pairs={{0,4},{4,8},{8,12},{12,0},{1,5},{5,9},{9,13},{13,1},{2,6},{6,10},{... | collective-permute-start | bytes 393224 | tf_op jit(solution)/shard_map/ppermute | solution.py:20
  273.7 18.7 %collective-permute-start.12 = (f32[32,1,4,256]{3,0,2,1:T(8,128)S(1)}, f32[32,1,4,256]{3,0,2,1:T(8,128)S(1)}, u32[]{:S(2)}, u32[]{:S(2)}) collective-permute-start(f32[32,1,4,256]{3,0,2,1:T(8,128)S(1)} %get-tuple-element.29), channel_id=1, source_target_pairs={{4,0},{8,4},{12,8},{0,12},{5,1},{9,5},{13,9},{1,13},{6,2},{10,6},{... | collective-permute-start | bytes 393224 | tf_op jit(solution)/shard_map/ppermute | solution.py:22
  292.3 1.9 copy-start.3
  292.4 1.5 collective-permute-start.14
  292.8 1.4 collective-permute-start.15
  (7 other events, 6.5 us)
Sparse Core Ops, SparseCore 0:
  10.1 23.9 all-gather.5
